TPU v7x, 32 devices: a whole 2x2x4 slice. The times are simulated.
32 devices in a mesh: seg: 8 (over z, y), ctl: 4 (over x, core).
Axes of the slice: x: 2, y: 2, z: 4, core: 2. Of those that a mesh axis runs over, the one named last changes fastest.
Arguments:
- transition: float32 [8, 1024, 1024], P('seg'), may hold values from -1 to 1
- control_map: float32 [8, 1024, 256], P('seg'), may hold values from -1.5 to 1.5
- weights: float32 [8, 1024], P('seg'), may hold values from 0.01 to 0.5
Outputs:
- sensitivity: float32 [8, 1024, 2048], P('seg', None, 'ctl')
- hessian_tiles: float32 [4, 512, 512], P('ctl', 'seg')
All inputs are finite; a program needn't handle non-finite values.
Results may differ from a plain program's by a relative error of at most 0.0003.
Values sent between devices are 32-bit elements; how exact they have to be, the bound alone decides.
No kernel may reach another device: no remote copies, remote signals or barrier semaphores. Data moves between devices by JAX's collectives and lax.ppermute only.
A program may use at most 128 MiB of HBM per device.

v0:
```python
import jax
import jax.numpy as jnp
from jax import lax
from jax.sharding import PartitionSpec as P


def from_behind(value, axis, by):
    devices = lax.axis_size(axis)
    pairs = [(i, i + by) for i in range(devices) if 0 <= i + by < devices]
    return lax.ppermute(value, axis, pairs)


def matmul_hi(left, right):
    return jnp.dot(left, right, precision=lax.Precision.HIGHEST, preferred_element_type=jnp.float32)


def gather_matrix(m_cols):
    return lax.all_gather(m_cols, "ctl", axis=1, tiled=True)


def earlier_sens(sens_block, reach):
    return from_behind(sens_block, "seg", reach)


def local(transition, control_map, weights):
    own_trans = transition[0]
    own_input = control_map[0]
    weight_row = weights[0]
    nseg = lax.axis_size("seg")
    nctl = lax.axis_size("ctl")
    seg_pos = lax.axis_index("seg")
    ctl_pos = lax.axis_index("ctl")
    stride = nseg // (2 * nctl)
    shard_width = own_trans.shape[1] // nctl
    blocks = [
        jnp.where(seg_pos == (2 * ctl_pos + slot_idx) * stride, own_input, 0.0)
        for slot_idx in range(2)
    ]
    sens_block = jnp.concatenate(blocks, axis=1)
    m_cols = lax.dynamic_slice_in_dim(own_trans, ctl_pos * shard_width, shard_width, 1)
    levels = (nseg - 1).bit_length()
    for level_idx in range(levels):
        reach = 1 << level_idx
        active = seg_pos >= reach
        is_last = level_idx == levels - 1
        own_whole = own_trans if level_idx == 0 else gather_matrix(m_cols)
        if is_last:
            prior_c = earlier_sens(sens_block, reach)
        else:
            prior_m, prior_c = from_behind((m_cols, sens_block), "seg", reach)
            m_cols = jnp.where(active, matmul_hi(own_whole, prior_m), m_cols)
        sens_block = jnp.where(active, matmul_hi(own_whole, prior_c) + sens_block, sens_block)
    weighted = sens_block * weight_row[:, None]
    hess_tile = lax.dot_general(
        sens_block,
        weighted,
        (((0,), (0,)), ((), ())),
        precision=lax.Precision.HIGHEST,
        preferred_element_type=jnp.float32,
    )
    summed = lax.psum(hess_tile, "seg")
    row_count = hess_tile.shape[0] // nseg
    hess_rows = lax.dynamic_slice_in_dim(summed, seg_pos * row_count, row_count, 0)
    return (sens_block[None], hess_rows[None])


def solution(mesh):
    return jax.shard_map(
        local,
        mesh=mesh,
        in_specs=(P("seg", None, None), P("seg", None, None), P("seg", None)),
        out_specs=(P("seg", None, "ctl"), P("ctl", "seg", None)),
        check_vma=False,
    )
```

profile of v0, /device:TPU:0, one launch (start us, length us, event | category | flops | bytes accessed | tf_op | source)
XLA Modules:
  0.0 375.8 jit_solution(13403189669114967752)
XLA Ops:
  7.2 0.0 all-gather.3.cloned.1.call-start
  7.2 1.3 constant_dynamic-slice_fusion
  8.5 0.3 copy.5
  8.9 5.0 %collective-permute-start = (f32[1024,256]{0,1:T(8,128)S(1)}, f32[1024,256]{0,1:T(8,128)S(1)}, u32[]{:S(2)}, u32[]{:S(2)}) collective-permute-start(f32[1024,256]{0,1:T(8,128)S(1)} %bitcast.37), channel_id=1, source_target_pairs={{0,4},{4,8},{8,12},{12,16},{16,20},{20,24},{24,28},{1,5},{5,9},{9,... | collective-permute-start | bytes 3145736 | tf_op jit(solution)/shard_map/ppermute | solution.py:10
  13.8 22.3 %collective-permute-done = f32[1024,256]{0,1:T(8,128)S(1)} collective-permute-done((f32[1024,256]{0,1:T(8,128)S(1)}, f32[1024,256]{0,1:T(8,128)S(1)}, u32[]{:S(2)}, u32[]{:S(2)}) %collective-permute-start) | collective-permute-done | bytes 1048608 | tf_op jit(solution)/shard_map/ppermute | solution.py:10
  36.2 6.9 %fusion.11 = f32[1024,256]{0,1:T(8,128)} fusion(f32[1024,256]{0,1:T(8,128)S(1)} %collective-permute-done, f32[1,1024,1024]{2,1,0:T(8,128)} %param.3, pred[]{:T(512)S(6)} %ge.11, f32[1,1024,256]{1,2,0:T(8,128)S(1)} %copy.5), kind=kOutput, calls=%fused_computation.11 | convolution fusion | flops 3221487616 | bytes 7340033 | tf_op jit(solution)/shard_map/dot_general | solution.py:14
  43.0 0.0 all-gather.3.cloned.1.call-update
  43.1 0.0 all-gather.5.cloned.1.call-start
  43.1 1.3 copy.6
  44.4 6.4 %collective-permute-start.1 = (f32[1024,256]{0,1:T(8,128)S(1)}, f32[1024,256]{0,1:T(8,128)}, u32[]{:S(2)}, u32[]{:S(2)}) collective-permute-start(f32[1024,256]{0,1:T(8,128)S(1)} %copy-done.1), channel_id=1, source_target_pairs={{0,8},{4,12},{8,16},{12,20},{16,24},{20,28},{1,9},{5,13},{9,17},{1... | collective-permute-start | bytes 3145736 | tf_op jit(solution)/shard_map/ppermute | solution.py:10
  50.8 1.6 select_bitcast_fusion.1
  52.4 1.5 pad_maximum_fusion
  53.8 3.8 %collective-permute-start.2 = (f32[1024,512]{0,1:T(8,128)}, f32[1024,512]{0,1:T(8,128)}, u32[]{:S(2)}, u32[]{:S(2)}) collective-permute-start(f32[1024,512]{0,1:T(8,128)} %pad_maximum_fusion), channel_id=1, source_target_pairs={{0,4},{4,8},{8,12},{12,16},{16,20},{20,24},{24,28},{1,5},{5,9},{9,... | collective-permute-start | bytes 6291464 | tf_op jit(solution)/shard_map/ppermute | solution.py:10
  57.6 13.7 %collective-permute-done.1 = f32[1024,256]{0,1:T(8,128)} collective-permute-done((f32[1024,256]{0,1:T(8,128)S(1)}, f32[1024,256]{0,1:T(8,128)}, u32[]{:S(2)}, u32[]{:S(2)}) %collective-permute-start.1) | collective-permute-done | bytes 1048608 | tf_op jit(solution)/shard_map/ppermute | solution.py:10
  71.3 8.6 %all-gather.3.cloned.1.call-done = f32[1024,1024]{0,1:T(8,128)} async-done(((f32[1024,256]{0,1:T(8,128)}), f32[1024,1024]{0,1:T(8,128)}) %all-gather.3.cloned.1.call-update) | async-done | bytes 4194320 | tf_op jit(solution)/shard_map/all_gather | solution.py:18
  79.9 7.3 %convolution_select_fusion = f32[1024,256]{0,1:T(8,128)} fusion(f32[1024,256]{0,1:T(8,128)S(1)} %copy-done.1, f32[1024,1024]{0,1:T(8,128)} %all-gather.3.cloned.1.call-done, f32[1024,256]{0,1:T(8,128)} %collective-permute-done.1, pred[]{:T(512)S(6)} %ge.10), kind=kOutput, calls=%fused_computation.12 | convolution fusion | flops 3221487616 | bytes 7340033 | tf_op jit(solution)/shard_map/dot_general | solution.py:14
  87.1 0.0 all-gather.5.cloned.1.call-update
  87.1 0.2 all-reduce.2.cloned.1.call-start
  87.4 12.9 %collective-permute-done.2 = f32[1024,512]{0,1:T(8,128)} collective-permute-done((f32[1024,512]{0,1:T(8,128)}, f32[1024,512]{0,1:T(8,128)}, u32[]{:S(2)}, u32[]{:S(2)}) %collective-permute-start.2) | collective-permute-done | bytes 2097184 | tf_op jit(solution)/shard_map/ppermute | solution.py:10
  100.3 10.0 %add_select_fusion.2 = f32[1024,512]{0,1:T(8,128)S(1)} fusion(f32[1024,512]{0,1:T(8,128)} %collective-permute-done.2, f32[1,1024,1024]{2,1,0:T(8,128)} %param.3, pred[]{:T(512)S(6)} %ge.11, f32[1024,256]{0,1:T(8,128)S(1)} %get-tuple-element.5, f32[1024,256]{0,1:T(8,128)S(1)} %get-tuple-element.4), kind=kOutput, calls=%fused_computation.8 | convolution fusion | flops 6444023808 | bytes 10485761 | tf_op jit(solution)/shard_map/dot_general | solution.py:14
  110.3 20.6 %collective-permute-start.3 = (f32[1024,512]{0,1:T(8,128)S(1)}, f32[1024,512]{0,1:T(8,128)S(1)}, u32[]{:S(2)}, u32[]{:S(2)}) collective-permute-start(f32[1024,512]{0,1:T(8,128)S(1)} %add_select_fusion.2), channel_id=1, source_target_pairs={{0,8},{4,12},{8,16},{12,20},{16,24},{20,28},{1,9},{5,13},{9,17},{1... | collective-permute-start | bytes 6291464 | tf_op jit(solution)/shard_map/ppermute | solution.py:10
  131.0 43.0 %collective-permute-done.3 = f32[1024,512]{0,1:T(8,128)S(1)} collective-permute-done((f32[1024,512]{0,1:T(8,128)S(1)}, f32[1024,512]{0,1:T(8,128)S(1)}, u32[]{:S(2)}, u32[]{:S(2)}) %collective-permute-start.3) | collective-permute-done | bytes 2097184 | tf_op jit(solution)/shard_map/ppermute | solution.py:10
  174.0 7.0 %add_select_fusion.1 = f32[1024,512]{0,1:T(8,128)S(1)} fusion(f32[1024,512]{0,1:T(8,128)S(1)} %add_select_fusion.2, f32[1024,1024]{0,1:T(8,128)S(1)} %copy-done, f32[1024,512]{0,1:T(8,128)S(1)} %collective-permute-done.3, pred[]{:T(512)S(6)} %ge.10), kind=kOutput, calls=%fused_computation.7 | convolution fusion | flops 6443499520 | bytes 10485761 | tf_op jit(solution)/shard_map/dot_general | solution.py:14
  180.9 0.0 copy-start.2
  180.9 6.8 %collective-permute-start.4 = (f32[1024,512]{0,1:T(8,128)S(1)}, f32[1024,512]{0,1:T(8,128)}, u32[]{:S(2)}, u32[]{:S(2)}) collective-permute-start(f32[1024,512]{0,1:T(8,128)S(1)} %add_select_fusion.1), channel_id=1, source_target_pairs={{0,16},{4,20},{8,24},{12,28},{1,17},{5,21},{9,25},{13,29},{2,18},{... | collective-permute-start | bytes 6291464 | tf_op jit(solution)/shard_map/ppermute | solution.py:10
  187.7 41.0 %collective-permute-done.4 = f32[1024,512]{0,1:T(8,128)} collective-permute-done((f32[1024,512]{0,1:T(8,128)S(1)}, f32[1024,512]{0,1:T(8,128)}, u32[]{:S(2)}, u32[]{:S(2)}) %collective-permute-start.4) | collective-permute-done | bytes 2097184 | tf_op jit(solution)/shard_map/ppermute | solution.py:10
  228.7 9.8 %add_select_fusion = f32[1024,512]{0,1:T(8,128)S(1)} fusion(f32[1024,512]{0,1:T(8,128)} %copy-done.2, f32[1024,1024]{0,1:T(8,128)} %all-gather.5.cloned.1.call-done, f32[1024,512]{0,1:T(8,128)} %collective-permute-done.4, pred[]{:T(512)S(6)} %ge.9), kind=kOutput, calls=%fused_computation.6 | convolution fusion | flops 6443499520 | bytes 10485761 | tf_op jit(solution)/shard_map/dot_general | solution.py:14
  238.5 4.5 %fusion.4 = f32[512,512]{1,0:T(8,128)} fusion(f32[1024,512]{0,1:T(8,128)S(1)} %add_select_fusion, f32[1024]{0:T(1024)S(1)} %bitcast.38), kind=kOutput, calls=%fused_computation.4 | convolution fusion | flops 3221749760 | bytes 3149824 | tf_op jit(solution)/shard_map/dot_general | solution.py:54
  243.1 0.0 all-reduce.2.cloned.1.call-update
  243.1 1.8 copy.10
  244.9 122.8 %all-reduce.2.cloned.1.call-done = f32[512,512]{1,0:T(8,128)} async-done(((f32[512,512]{1,0:T(8,128)}), f32[512,512]{1,0:T(8,128)}) %all-reduce.2.cloned.1.call-update) | async-done | bytes 1048592 | tf_op jit(solution)/shard_map/psum | solution.py:61
  367.7 1.6 dynamic-slice_bitcast_fusion
  (10 shorter events, 0.0 us)
Async XLA Ops:
  7.2 72.7 %all-gather.3.cloned.1.call-start = ((), (), s32[]{:S(2)}) async-start(), calls=%async_computation | async-start | bytes 5242880 | tf_op jit(solution)/shard_map/all_gather | solution.py:18
  8.9 27.3 %collective-permute-start = (f32[1024,256]{0,1:T(8,128)S(1)}, f32[1024,256]{0,1:T(8,128)S(1)}, u32[]{:S(2)}, u32[]{:S(2)}) collective-permute-start(f32[1024,256]{0,1:T(8,128)S(1)} %bitcast.37), channel_id=1, source_target_pairs={{0,4},{4,8},{8,12},{12,16},{16,20},{20,24},{24,28},{1,5},{5,9},{9,... | collective-permute-start | bytes 3145736 | tf_op jit(solution)/shard_map/ppermute | solution.py:10
  13.8 29.3 %copy-start.3 = (f32[1,1024,256]{2,1,0:T(8,128)S(1)}, f32[1,1024,256]{2,1,0:T(8,128)}, u32[]{:S(2)}) copy-start(f32[1,1024,256]{2,1,0:T(8,128)} %param.4) | copy-start | bytes 3145732
  43.0 1.4 copy-start.1
  43.1 185.6 %all-gather.5.cloned.1.call-start = ((), (), s32[]{:S(2)}) async-start(), calls=%async_computation.1 | async-start | bytes 5242880 | tf_op jit(solution)/shard_map/all_gather | solution.py:18
  44.4 26.9 %collective-permute-start.1 = (f32[1024,256]{0,1:T(8,128)S(1)}, f32[1024,256]{0,1:T(8,128)}, u32[]{:S(2)}, u32[]{:S(2)}) collective-permute-start(f32[1024,256]{0,1:T(8,128)S(1)} %copy-done.1), channel_id=1, source_target_pairs={{0,8},{4,12},{8,16},{12,20},{16,24},{20,28},{1,9},{5,13},{9,17},{1... | collective-permute-start | bytes 3145736 | tf_op jit(solution)/shard_map/ppermute | solution.py:10
  53.8 46.5 %collective-permute-start.2 = (f32[1024,512]{0,1:T(8,128)}, f32[1024,512]{0,1:T(8,128)}, u32[]{:S(2)}, u32[]{:S(2)}) collective-permute-start(f32[1024,512]{0,1:T(8,128)} %pad_maximum_fusion), channel_id=1, source_target_pairs={{0,4},{4,8},{8,12},{12,16},{16,20},{20,24},{24,28},{1,5},{5,9},{9,... | collective-permute-start | bytes 6291464 | tf_op jit(solution)/shard_map/ppermute | solution.py:10
  87.1 280.6 %all-reduce.2.cloned.1.call-start = ((), (), s32[]{:S(2)}) async-start(), calls=%async_computation.2 | async-start | bytes 2097152 | tf_op jit(solution)/shard_map/psum | solution.py:61
  100.3 73.7 %copy-start = (f32[1024,1024]{0,1:T(8,128)S(1)}, f32[1024,1024]{0,1:T(8,128)}, u32[]{:S(2)}) copy-start(f32[1024,1024]{0,1:T(8,128)} %all-gather.3.cloned.1.call-done) | copy-start | bytes 12582916
  110.3 63.6 %collective-permute-start.3 = (f32[1024,512]{0,1:T(8,128)S(1)}, f32[1024,512]{0,1:T(8,128)S(1)}, u32[]{:S(2)}, u32[]{:S(2)}) collective-permute-start(f32[1024,512]{0,1:T(8,128)S(1)} %add_select_fusion.2), channel_id=1, source_target_pairs={{0,8},{4,12},{8,16},{12,20},{16,24},{20,28},{1,9},{5,13},{9,17},{1... | collective-permute-start | bytes 6291464 | tf_op jit(solution)/shard_map/ppermute | solution.py:10
  180.9 47.7 %copy-start.2 = (f32[1024,512]{0,1:T(8,128)}, f32[1024,512]{0,1:T(8,128)S(1)}, u32[]{:S(2)}) copy-start(f32[1024,512]{0,1:T(8,128)S(1)} %add_select_fusion.1) | copy-start | bytes 6291460
  180.9 47.7 %collective-permute-start.4 = (f32[1024,512]{0,1:T(8,128)S(1)}, f32[1024,512]{0,1:T(8,128)}, u32[]{:S(2)}, u32[]{:S(2)}) collective-permute-start(f32[1024,512]{0,1:T(8,128)S(1)} %add_select_fusion.1), channel_id=1, source_target_pairs={{0,16},{4,20},{8,24},{12,28},{1,17},{5,21},{9,25},{13,29},{2,18},{... | collective-permute-start | bytes 6291464 | tf_op jit(solution)/shard_map/ppermute | solution.py:10
  187.7 50.8 %copy-start.4 = (f32[1,1024]{1,0:T(1,128)S(1)}, f32[1,1024]{1,0:T(1,128)}, u32[]{:S(2)}) copy-start(f32[1,1024]{1,0:T(1,128)} %param.5) | copy-start | bytes 12292
Sparse Core Ops, SparseCore 0:
  43.2 36.6 all-gather.2
  87.3 34.4 all-gather.4
  243.2 124.4 all-reduce.1
where the time goes:
time: 376 us
  waiting for transfers between devices  264 us (70%)
  matrix products  45.5 us (12%)
  starting transfers between devices  42.8 us (11%)
  between operations  13.9 us (4%)
  local copies, waits for them, and re-layouts  6.34 us (2%)
    ppermute x5, waiting for transfers between devices, from_behind(): return lax.ppermute(value, axis, pairs)  133 us
    psum x1, waiting for transfers between devices, local(): summed = lax.psum(hess_tile, 'seg')  123 us
    ppermute x5, starting transfers between devices, from_behind(): return lax.ppermute(value, axis, pairs)  42.5 us
    dot_general x5, matrix products, matmul_hi(): jnp.dot(left, right, precision=lax.Precision.HIGHEST, preferred_element_t...  40.9 us
    all_gather x2, waiting for transfers between devices, gather_matrix(): return lax.all_gather(m_cols, 'ctl', axis=1, tiled=True)  8.56 us
  transfers between devices with their start and end apart: 8, of which 7 were waited for; matrix products, arithmetic and copies ran while one was open for 8% of the time, Pallas kernels for 0%

commit v1 on v0

--- a/solution.py
+++ b/solution.py
@@ -58,7 +58,7 @@
         precision=lax.Precision.HIGHEST,
         preferred_element_type=jnp.float32,
     )
-    summed = lax.psum(hess_tile, "seg")
+    summed = jnp.sum(lax.all_gather(hess_tile, "seg"), axis=0)
     row_count = hess_tile.shape[0] // nseg
     hess_rows = lax.dynamic_slice_in_dim(summed, seg_pos * row_count, row_count, 0)
     return (sens_block[None], hess_rows[None])

time: 376 us -> 426 us (1.13)
  waiting for transfers between devices: 264 us -> 310 us
  other arithmetic: 3.03 us -> 7.52 us
    all_gather x0 -> x1, waiting for transfers between devices: none -> 169 us  [local(): summed = jnp.sum(lax.all_gather(hess_tile, 'seg'), axis=0)]
    psum x1 -> x0, waiting for transfers between devices: 123 us -> none  [local(): summed = lax.psum(hess_tile, 'seg')]
    reduce_sum x0 -> x1, other arithmetic: none -> 4.49 us  [local(): summed = jnp.sum(lax.all_gather(hess_tile, 'seg'), axis=0)]
  transfers between devices with their start and end apart: 8 -> 8, of which waited for: 7 -> 7; matrix products, arithmetic and copies ran while one was open for 8% -> 7% of each run, Pallas kernels for 0% -> 0%
where the time goes in v1:
time: 426 us
  waiting for transfers between devices  310 us (73%)
  matrix products  45.5 us (11%)
  starting transfers between devices  42.8 us (10%)
  between operations  13.9 us (3%)
  other arithmetic  7.52 us (2%)
  local copies, waits for them, and re-layouts  5.45 us (1%)
    all_gather x1, waiting for transfers between devices, local(): summed = jnp.sum(lax.all_gather(hess_tile, 'seg'), axis=0)  169 us
    ppermute x5, waiting for transfers between devices, from_behind(): return lax.ppermute(value, axis, pairs)  133 us
    ppermute x5, starting transfers between devices, from_behind(): return lax.ppermute(value, axis, pairs)  42.5 us
    dot_general x5, matrix products, matmul_hi(): jnp.dot(left, right, precision=lax.Precision.HIGHEST, preferred_element_t...  40.9 us
    all_gather x2, waiting for transfers between devices, gather_matrix(): return lax.all_gather(m_cols, 'ctl', axis=1, tiled=True)  8.56 us
  transfers between devices with their start and end apart: 8, of which 7 were waited for; matrix products, arithmetic and copies ran while one was open for 7% of the time, Pallas kernels for 0%

profile of v1, /device:TPU:0, one launch (start us, length us, event | category | flops | bytes accessed | tf_op | source)
XLA Modules:
  0.0 425.6 jit_solution(9076052671332446366)
XLA Ops:
  7.2 0.0 all-gather.5.cloned.1.call-start
  7.2 1.3 constant_dynamic-slice_fusion
  8.5 0.3 copy.5
  8.9 5.0 %collective-permute-start = (f32[1024,256]{0,1:T(8,128)S(1)}, f32[1024,256]{0,1:T(8,128)S(1)}, u32[]{:S(2)}, u32[]{:S(2)}) collective-permute-start(f32[1024,256]{0,1:T(8,128)S(1)} %bitcast.39), channel_id=1, source_target_pairs={{0,4},{4,8},{8,12},{12,16},{16,20},{20,24},{24,28},{1,5},{5,9},{9,... | collective-permute-start | bytes 3145736 | tf_op jit(solution)/shard_map/ppermute | solution.py:10
  13.8 22.3 %collective-permute-done = f32[1024,256]{0,1:T(8,128)S(1)} collective-permute-done((f32[1024,256]{0,1:T(8,128)S(1)}, f32[1024,256]{0,1:T(8,128)S(1)}, u32[]{:S(2)}, u32[]{:S(2)}) %collective-permute-start) | collective-permute-done | bytes 1048608 | tf_op jit(solution)/shard_map/ppermute | solution.py:10
  36.2 6.9 %fusion.11 = f32[1024,256]{0,1:T(8,128)} fusion(f32[1024,256]{0,1:T(8,128)S(1)} %collective-permute-done, f32[1,1024,1024]{2,1,0:T(8,128)} %param.3, pred[]{:T(512)S(6)} %ge.11, f32[1,1024,256]{1,2,0:T(8,128)S(1)} %copy.5), kind=kOutput, calls=%fused_computation.11 | convolution fusion | flops 3221487616 | bytes 7340033 | tf_op jit(solution)/shard_map/dot_general | solution.py:14
  43.0 0.0 all-gather.5.cloned.1.call-update
  43.1 0.0 all-gather.7.cloned.1.call-start
  43.1 1.3 copy.6
  44.4 6.4 %collective-permute-start.1 = (f32[1024,256]{0,1:T(8,128)S(1)}, f32[1024,256]{0,1:T(8,128)}, u32[]{:S(2)}, u32[]{:S(2)}) collective-permute-start(f32[1024,256]{0,1:T(8,128)S(1)} %copy-done.1), channel_id=1, source_target_pairs={{0,8},{4,12},{8,16},{12,20},{16,24},{20,28},{1,9},{5,13},{9,17},{1... | collective-permute-start | bytes 3145736 | tf_op jit(solution)/shard_map/ppermute | solution.py:10
  50.8 1.6 select_bitcast_fusion.1
  52.4 1.5 pad_maximum_fusion
  53.8 3.8 collective-permute-start.2
  57.6 13.7 %collective-permute-done.1 = f32[1024,256]{0,1:T(8,128)} collective-permute-done((f32[1024,256]{0,1:T(8,128)S(1)}, f32[1024,256]{0,1:T(8,128)}, u32[]{:S(2)}, u32[]{:S(2)}) %collective-permute-start.1) | collective-permute-done | bytes 1048608 | tf_op jit(solution)/shard_map/ppermute | solution.py:10
  71.3 8.6 %all-gather.5.cloned.1.call-done = f32[1024,1024]{0,1:T(8,128)} async-done(((f32[1024,256]{0,1:T(8,128)}), f32[1024,1024]{0,1:T(8,128)}) %all-gather.5.cloned.1.call-update) | async-done | bytes 4194320 | tf_op jit(solution)/shard_map/all_gather | solution.py:18
  79.9 7.3 %convolution_select_fusion = f32[1024,256]{0,1:T(8,128)} fusion(f32[1024,256]{0,1:T(8,128)S(1)} %copy-done.1, f32[1024,1024]{0,1:T(8,128)} %all-gather.5.cloned.1.call-done, f32[1024,256]{0,1:T(8,128)} %collective-permute-done.1, pred[]{:T(512)S(6)} %ge.10), kind=kOutput, calls=%fused_computation.12 | convolution fusion | flops 3221487616 | bytes 7340033 | tf_op jit(solution)/shard_map/dot_general | solution.py:14
  87.1 0.0 all-gather.7.cloned.1.call-update
  87.1 0.2 all-gather.9.cloned.1.call-start
  87.4 12.9 %collective-permute-done.2 = f32[1024,512]{0,1:T(8,128)} collective-permute-done((f32[1024,512]{0,1:T(8,128)}, f32[1024,512]{0,1:T(8,128)}, u32[]{:S(2)}, u32[]{:S(2)}) %collective-permute-start.2) | collective-permute-done | bytes 2097184 | tf_op jit(solution)/shard_map/ppermute | solution.py:10
  100.3 10.0 %add_select_fusion.2 = f32[1024,512]{0,1:T(8,128)S(1)} fusion(f32[1024,512]{0,1:T(8,128)} %collective-permute-done.2, f32[1,1024,1024]{2,1,0:T(8,128)} %param.3, pred[]{:T(512)S(6)} %ge.11, f32[1024,256]{0,1:T(8,128)S(1)} %get-tuple-element.5, f32[1024,256]{0,1:T(8,128)S(1)} %get-tuple-element.4), kind=kOutput, calls=%fused_computation.8 | convolution fusion | flops 6444023808 | bytes 10485761 | tf_op jit(solution)/shard_map/dot_general | solution.py:14
  110.3 20.6 %collective-permute-start.3 = (f32[1024,512]{0,1:T(8,128)S(1)}, f32[1024,512]{0,1:T(8,128)S(1)}, u32[]{:S(2)}, u32[]{:S(2)}) collective-permute-start(f32[1024,512]{0,1:T(8,128)S(1)} %add_select_fusion.2), channel_id=1, source_target_pairs={{0,8},{4,12},{8,16},{12,20},{16,24},{20,28},{1,9},{5,13},{9,17},{1... | collective-permute-start | bytes 6291464 | tf_op jit(solution)/shard_map/ppermute | solution.py:10
  131.0 43.0 %collective-permute-done.3 = f32[1024,512]{0,1:T(8,128)S(1)} collective-permute-done((f32[1024,512]{0,1:T(8,128)S(1)}, f32[1024,512]{0,1:T(8,128)S(1)}, u32[]{:S(2)}, u32[]{:S(2)}) %collective-permute-start.3) | collective-permute-done | bytes 2097184 | tf_op jit(solution)/shard_map/ppermute | solution.py:10
  174.0 7.0 %add_select_fusion.1 = f32[1024,512]{0,1:T(8,128)S(1)} fusion(f32[1024,512]{0,1:T(8,128)S(1)} %add_select_fusion.2, f32[1024,1024]{0,1:T(8,128)S(1)} %copy-done, f32[1024,512]{0,1:T(8,128)S(1)} %collective-permute-done.3, pred[]{:T(512)S(6)} %ge.10), kind=kOutput, calls=%fused_computation.7 | convolution fusion | flops 6443499520 | bytes 10485761 | tf_op jit(solution)/shard_map/dot_general | solution.py:14
  180.9 6.8 %collective-permute-start.4 = (f32[1024,512]{0,1:T(8,128)S(1)}, f32[1024,512]{0,1:T(8,128)}, u32[]{:S(2)}, u32[]{:S(2)}) collective-permute-start(f32[1024,512]{0,1:T(8,128)S(1)} %add_select_fusion.1), channel_id=1, source_target_pairs={{0,16},{4,20},{8,24},{12,28},{1,17},{5,21},{9,25},{13,29},{2,18},{... | collective-permute-start | bytes 6291464 | tf_op jit(solution)/shard_map/ppermute | solution.py:10
  187.7 41.0 %collective-permute-done.4 = f32[1024,512]{0,1:T(8,128)} collective-permute-done((f32[1024,512]{0,1:T(8,128)S(1)}, f32[1024,512]{0,1:T(8,128)}, u32[]{:S(2)}, u32[]{:S(2)}) %collective-permute-start.4) | collective-permute-done | bytes 2097184 | tf_op jit(solution)/shard_map/ppermute | solution.py:10
  228.7 9.8 %add_select_fusion = f32[1024,512]{0,1:T(8,128)S(1)} fusion(f32[1024,512]{0,1:T(8,128)} %copy-done.2, f32[1024,1024]{0,1:T(8,128)} %all-gather.7.cloned.1.call-done, f32[1024,512]{0,1:T(8,128)} %collective-permute-done.4, pred[]{:T(512)S(6)} %ge.9), kind=kOutput, calls=%fused_computation.6 | convolution fusion | flops 6443499520 | bytes 10485761 | tf_op jit(solution)/shard_map/dot_general | solution.py:14
  238.5 4.6 %fusion.4 = f32[512,512]{1,0:T(8,128)} fusion(f32[1024,512]{0,1:T(8,128)S(1)} %add_select_fusion, f32[1024]{0:T(1024)S(1)} %bitcast.40), kind=kOutput, calls=%fused_computation.4 | convolution fusion | flops 3221749760 | bytes 3149824 | tf_op jit(solution)/shard_map/dot_general | solution.py:54
  243.1 0.0 all-gather.9.cloned.1.call-update
  243.1 1.8 copy.10
  245.0 168.9 %all-gather.9.cloned.1.call-done = f32[4096,512]{1,0:T(8,128)} async-done(((f32[512,512]{1,0:T(8,128)}), f32[4096,512]{1,0:T(8,128)}) %all-gather.9.cloned.1.call-update) | async-done | bytes 8388624 | tf_op jit(solution)/shard_map/all_gather | solution.py:61
  413.9 4.5 %reduce_sum.9 = f32[512,512]{1,0:T(8,128)S(1)} reduce(f32[8,512,512]{2,1,0:T(8,128)} %bitcast.38, f32[]{:T(128)} %constant.25.clone.1), dimensions={0}, to_apply=%region_0.1 | reduce | flops 1835008 | bytes 9437188 | tf_op jit(solution)/shard_map/reduce_sum | solution.py:61
  418.4 0.7 dynamic-slice_bitcast_fusion
  (11 shorter events, 0.0 us)
Async XLA Ops:
  7.2 72.7 %all-gather.5.cloned.1.call-start = ((), (), s32[]{:S(2)}) async-start(), calls=%async_computation | async-start | bytes 5242880 | tf_op jit(solution)/shard_map/all_gather | solution.py:18
  8.9 27.3 %collective-permute-start = (f32[1024,256]{0,1:T(8,128)S(1)}, f32[1024,256]{0,1:T(8,128)S(1)}, u32[]{:S(2)}, u32[]{:S(2)}) collective-permute-start(f32[1024,256]{0,1:T(8,128)S(1)} %bitcast.39), channel_id=1, source_target_pairs={{0,4},{4,8},{8,12},{12,16},{16,20},{20,24},{24,28},{1,5},{5,9},{9,... | collective-permute-start | bytes 3145736 | tf_op jit(solution)/shard_map/ppermute | solution.py:10
  13.8 29.3 %copy-start.3 = (f32[1,1024,256]{2,1,0:T(8,128)S(1)}, f32[1,1024,256]{2,1,0:T(8,128)}, u32[]{:S(2)}) copy-start(f32[1,1024,256]{2,1,0:T(8,128)} %param.4) | copy-start | bytes 3145732
  43.0 1.4 copy-start.1
  43.1 185.6 %all-gather.7.cloned.1.call-start = ((), (), s32[]{:S(2)}) async-start(), calls=%async_computation.1 | async-start | bytes 5242880 | tf_op jit(solution)/shard_map/all_gather | solution.py:18
  44.4 26.9 %collective-permute-start.1 = (f32[1024,256]{0,1:T(8,128)S(1)}, f32[1024,256]{0,1:T(8,128)}, u32[]{:S(2)}, u32[]{:S(2)}) collective-permute-start(f32[1024,256]{0,1:T(8,128)S(1)} %copy-done.1), channel_id=1, source_target_pairs={{0,8},{4,12},{8,16},{12,20},{16,24},{20,28},{1,9},{5,13},{9,17},{1... | collective-permute-start | bytes 3145736 | tf_op jit(solution)/shard_map/ppermute | solution.py:10
  53.8 46.5 %collective-permute-start.2 = (f32[1024,512]{0,1:T(8,128)}, f32[1024,512]{0,1:T(8,128)}, u32[]{:S(2)}, u32[]{:S(2)}) collective-permute-start(f32[1024,512]{0,1:T(8,128)} %pad_maximum_fusion), channel_id=1, source_target_pairs={{0,4},{4,8},{8,12},{12,16},{16,20},{20,24},{24,28},{1,5},{5,9},{9,... | collective-permute-start | bytes 6291464 | tf_op jit(solution)/shard_map/ppermute | solution.py:10
  87.1 326.7 %all-gather.9.cloned.1.call-start = ((), (), s32[]{:S(2)}) async-start(), calls=%async_computation.2 | async-start | bytes 9437184 | tf_op jit(solution)/shard_map/all_gather | solution.py:61
  100.3 73.7 %copy-start = (f32[1024,1024]{0,1:T(8,128)S(1)}, f32[1024,1024]{0,1:T(8,128)}, u32[]{:S(2)}) copy-start(f32[1024,1024]{0,1:T(8,128)} %all-gather.5.cloned.1.call-done) | copy-start | bytes 12582916
  110.3 63.6 %collective-permute-start.3 = (f32[1024,512]{0,1:T(8,128)S(1)}, f32[1024,512]{0,1:T(8,128)S(1)}, u32[]{:S(2)}, u32[]{:S(2)}) collective-permute-start(f32[1024,512]{0,1:T(8,128)S(1)} %add_select_fusion.2), channel_id=1, source_target_pairs={{0,8},{4,12},{8,16},{12,20},{16,24},{20,28},{1,9},{5,13},{9,17},{1... | collective-permute-start | bytes 6291464 | tf_op jit(solution)/shard_map/ppermute | solution.py:10
  180.9 47.7 %copy-start.2 = (f32[1024,512]{0,1:T(8,128)}, f32[1024,512]{0,1:T(8,128)S(1)}, u32[]{:S(2)}) copy-start(f32[1024,512]{0,1:T(8,128)S(1)} %add_select_fusion.1) | copy-start | bytes 6291460
  180.9 47.7 %collective-permute-start.4 = (f32[1024,512]{0,1:T(8,128)S(1)}, f32[1024,512]{0,1:T(8,128)}, u32[]{:S(2)}, u32[]{:S(2)}) collective-permute-start(f32[1024,512]{0,1:T(8,128)S(1)} %add_select_fusion.1), channel_id=1, source_target_pairs={{0,16},{4,20},{8,24},{12,28},{1,17},{5,21},{9,25},{13,29},{2,18},{... | collective-permute-start | bytes 6291464 | tf_op jit(solution)/shard_map/ppermute | solution.py:10
  187.7 50.8 %copy-start.4 = (f32[1,1024]{1,0:T(1,128)S(1)}, f32[1,1024]{1,0:T(1,128)}, u32[]{:S(2)}) copy-start(f32[1,1024]{1,0:T(1,128)} %param.5) | copy-start | bytes 12292
Sparse Core Ops, SparseCore 0:
  43.2 36.6 all-gather.4
  87.3 34.4 all-gather.6
  243.3 170.5 all-gather.8
